TPU v7x, 32 devices: a whole 2x2x4 slice. The times are simulated.
32 devices in a mesh: lon: 4 (over x, core), lat: 2 (over y), frame: 4 (over z).
Axes of the slice: x: 2, y: 2, z: 4, core: 2. Of those that a mesh axis runs over, the one named last changes fastest.
Arguments:
- features: bfloat16 [4, 128, 64, 256], P('frame', 'lon', 'lat'), may hold values from -6 to 6
- cotangent: bfloat16 [4, 128, 64, 162], P('frame', 'lon', 'lat'), may hold values from -6 to 6
Outputs:
- grads: bfloat16 [4, 128, 64, 256], P('frame', 'lon', 'lat')
All inputs are finite; a program needn't handle non-finite values.
Results may differ from a plain program's by a relative error of at most 0.0023.
Values may be sent and summed in bfloat16 or wider, within the bound.
A program may use at most 64 MiB of HBM per device.

v0:
```python
import jax
import jax.numpy as jnp
import numpy as np
from jax import lax
from jax.experimental import pallas as pl
from jax.experimental.pallas import tpu as pltpu
from jax.sharding import PartitionSpec as P

LEVELS = 2
RAD = 4
RIM = 8
ACROSS = 2 * RAD + 1
HALF = 512


def extended_2(array, sides, width, wrap):
    for axis, dim in sides:
        size, length = (lax.axis_size(axis), array.shape[dim])
        up = [(i, (i + 1) % size) for i in range(size if wrap else size - 1)]
        down = [(j, i) for i, j in up]
        last = lax.slice_in_dim(array, length - width, length, axis=dim)
        first = lax.slice_in_dim(array, 0, width, axis=dim)
        before = lax.ppermute(last, axis, up)
        after = lax.ppermute(first, axis, down)
        array = jnp.concatenate([before, array, after], axis=dim)
    return array


def from_behind(value, axis, steps):
    count = lax.axis_size(axis)
    first, last = (max(0, -steps), min(count, count - steps))
    return lax.ppermute(value, axis, [(source, source + steps) for source in range(first, last)])


def spreader(rows):
    out = np.zeros((LEVELS * ACROSS * ACROSS, LEVELS * HALF), np.float32)
    for a in range(ACROSS):
        for b in range(ACROSS):
            out[a * ACROSS + b, a * rows + RAD + b] = 1
            out[ACROSS * ACROSS + a * ACROSS + b, HALF + a * rows + 2 * b] = 1
    return jnp.asarray(out).astype(jnp.bfloat16)


def sheared(spread):
    return pltpu.roll(spread, 0, 1, stride=1, stride_axis=0).astype(jnp.bfloat16)


def pair_sum(value):
    rows = value.shape[0]
    odd = lax.broadcasted_iota(jnp.int32, value.shape, 0) % 2 == 1
    return value + jnp.where(odd, pltpu.roll(value, 1, 0), pltpu.roll(value, rows - 1, 0))


def own_kernel(cot_ref, ext_ref, spread_ref, out_ref, pool_ref):
    cols, rows, chans = out_ref.shape
    wide = rows + 2 * RIM
    depth = ACROSS * wide

    @pl.loop(0, (cols + 2 * RIM) // 2)
    def _(pos):
        both = ext_ref[2 * pos].astype(jnp.float32) + ext_ref[2 * pos + 1].astype(jnp.float32)
        pool_ref[pos] = (pair_sum(both) * 0.25).astype(jnp.bfloat16)

    @pl.loop(0, cols)
    def _(x):
        spread = jnp.dot(cot_ref[x], spread_ref[...], preferred_element_type=jnp.float32)
        near = sheared(spread[:, :HALF])[:, :depth]
        far = sheared(spread[:, HALF:])[:, :depth]
        keys = ext_ref[pl.ds(x + RAD, ACROSS)].reshape(depth, chans)
        pooled = pool_ref[pl.ds(x // 2, ACROSS)].reshape(depth, chans)
        total = jnp.dot(near, keys, preferred_element_type=jnp.float32)
        total = total + jnp.dot(far, pooled, preferred_element_type=jnp.float32)
        out_ref[x] = total * chans ** (-0.5)


def back_kernel(ext_ref, spread_ref, out_ref, near_ref, far_ref):
    cols, rows, chans = out_ref.shape
    wide = rows + 2 * RIM
    contract = (((0,), (0,)), ((), ()))

    @pl.loop(0, cols + 4 * RIM)
    def _(pos):
        near_ref[pos] = jnp.zeros((rows, chans), jnp.float32)
        far_ref[pos] = jnp.zeros((rows, chans), jnp.float32)

    @pl.loop(0, cols + 2 * RIM)
    def _(x):
        feats = ext_ref[x, :, :chans]
        spread = jnp.dot(ext_ref[x, :, chans:], spread_ref[...], preferred_element_type=jnp.float32)
        near = lax.dot_general(sheared(spread[:, :HALF]), feats, contract, preferred_element_type=jnp.float32)
        far = lax.dot_general(sheared(spread[:, HALF:]), feats, contract, preferred_element_type=jnp.float32)
        for a in range(ACROSS):
            begin = a * wide + 2 * RIM
            near_ref[x + a + RAD] += near[begin : begin + rows]
            far_ref[x + 2 * a] += far[begin : begin + rows]

    @pl.loop(0, cols // 2)
    def _(pos):
        u = 2 * pos + 2 * RIM
        both = pair_sum(far_ref[u] + far_ref[u + 1]) * 0.25
        out_ref[2 * pos] = (near_ref[u] + both) * chans ** (-0.5)
        out_ref[2 * pos + 1] = (near_ref[u + 1] + both) * chans ** (-0.5)


def local_call(kernel, cols, rows, chans, scratch, flops, *args):
    vmem = pl.BlockSpec(memory_space=pltpu.VMEM)
    return pl.pallas_call(
        kernel,
        out_shape=jax.ShapeDtypeStruct((cols, rows, chans), jnp.float32),
        in_specs=[vmem] * len(args),
        out_specs=vmem,
        scratch_shapes=scratch,
        cost_estimate=pl.CostEstimate(flops=flops, bytes_accessed=4 << 20, transcendentals=0),
        compiler_params=pltpu.CompilerParams(vmem_limit_bytes=40 << 20),
    )(*args)


def extend(stacked):
    beside_all = extended_2(stacked, (("lon", 0),), RIM, True)
    return extended_2(beside_all, (("lat", 1),), RIM, False)


def body(features, cotangent):
    _, cols, rows, chans = features.shape
    wide = rows + 2 * RIM
    spread = spreader(wide)
    following = from_behind(features, "frame", -1)
    query_ext = extend(jnp.concatenate([features[0], cotangent[0]], axis=2))
    next_ext = extend(following[0])
    wider = pltpu.VMEM((cols + 4 * RIM, rows, chans), jnp.float32)
    key_part = local_call(back_kernel, cols, rows, chans, [wider, wider], 10**10, query_ext, spread)
    carried = from_behind(key_part, "frame", 1)
    pool = pltpu.VMEM((cols // 2 + RIM, wide, chans), jnp.bfloat16)
    own = local_call(own_kernel, cols, rows, chans, [pool], 10**10, cotangent[0], next_ext, spread)
    return (own + carried).astype(jnp.bfloat16)[None]


def solution(mesh):
    placed = (P("frame", "lon", "lat", None), P("frame", "lon", "lat", None))
    return jax.shard_map(
        body, mesh=mesh, in_specs=placed, out_specs=P("frame", "lon", "lat", None), check_vma=False
    )
```

profile of v0, /device:TPU:0, one launch (start us, length us, event | category | flops | bytes accessed | tf_op | source)
XLA Modules:
  0.0 92.1 jit_solution(16971207714747109549)
XLA Ops:
  0.0 0.0 copy-start.2
  0.0 0.0 copy-start
  0.0 1.4 %collective-permute-start = (bf16[1,32,32,256]{3,2,1,0:T(8,128)(2,1)}, bf16[1,32,32,256]{3,2,1,0:T(8,128)(2,1)S(1)}, u32[]{:S(2)}, u32[]{:S(2)}) collective-permute-start(bf16[1,32,32,256]{3,2,1,0:T(8,128)(2,1)} %param.3), channel_id=1, source_target_pairs={{1,0},{2,1},{3,2},{5,4},{6,5},{7,6},{9,8},{10,9},{11,10},{13,12},{... | collective-permute-start | bytes 1572872 | tf_op jit(solution)/shard_map/ppermute | solution.py:32
  1.4 1.2 %pad_maximum_fusion.7 = (bf16[8,32,418]{2,1,0:T(8,128)(2,1)S(1)}, bf16[8,32,418]{2,1,0:T(8,128)(2,1)S(1)}) fusion(bf16[32,32,162]{2,1,0:T(8,128)(2,1)} %bitcast.9, bf16[32,32,256]{2,1,0:T(8,128)(2,1)} %bitcast.13), kind=kLoop, calls=%fused_computation.9 | loop fusion | flops 856064 | bytes 1284096 | tf_op jit(solution)/shard_map/slice | solution.py:21
  2.6 0.5 collective-permute-start.5
  3.1 2.0 %collective-permute-start.6 = (bf16[8,32,418]{2,1,0:T(8,128)(2,1)S(1)}, bf16[8,32,418]{2,1,0:T(8,128)(2,1)S(1)}, u32[]{:S(2)}, u32[]{:S(2)}) collective-permute-start(bf16[8,32,418]{2,1,0:T(8,128)(2,1)S(1)} %get-tuple-element.8), channel_id=1, source_target_pairs={{8,0},{16,8},{24,16},{0,24},{9,1},{17,9},{25,17},{1,25},{10,2},{18... | collective-permute-start | bytes 642056 | tf_op jit(solution)/shard_map/ppermute | solution.py:24
  5.1 4.2 %collective-permute-done.5 = bf16[8,32,418]{2,1,0:T(8,128)(2,1)S(1)} collective-permute-done((bf16[8,32,418]{2,1,0:T(8,128)(2,1)S(1)}, bf16[8,32,418]{2,1,0:T(8,128)(2,1)S(1)}, u32[]{:S(2)}, u32[]{:S(2)}) %collective-permute-start.5) | collective-permute-done | bytes 214048 | tf_op jit(solution)/shard_map/ppermute | solution.py:23
  9.3 2.4 %collective-permute-done.6 = bf16[8,32,418]{2,1,0:T(8,128)(2,1)S(1)} collective-permute-done((bf16[8,32,418]{2,1,0:T(8,128)(2,1)S(1)}, bf16[8,32,418]{2,1,0:T(8,128)(2,1)S(1)}, u32[]{:S(2)}, u32[]{:S(2)}) %collective-permute-start.6) | collective-permute-done | bytes 214048 | tf_op jit(solution)/shard_map/ppermute | solution.py:24
  11.7 1.2 %pad_maximum_fusion.5 = (bf16[48,8,418]{2,1,0:T(8,128)(2,1)S(1)}, bf16[48,8,418]{2,1,0:T(8,128)(2,1)S(1)}) fusion(bf16[8,32,418]{2,1,0:T(8,128)(2,1)S(1)} %collective-permute-done.6, bf16[8,32,418]{2,1,0:T(8,128)(2,1)S(1)} %collective-permute-done.5, bf16[32,32,162]{2,1,0:T(8,128)(2,1)} %bitcast.10, bf16[32,32,256]{2,1,0:T(8,128)(2,1)} %bitcast.14), kind=kLoop, calls=%fused_computation.7 | loop fusion | flops 2568192 | bytes 1926144 | tf_op jit(solution)/shard_map/slice | solution.py:21
  12.9 3.4 %collective-permute-start.7 = (bf16[48,8,418]{2,1,0:T(8,128)(2,1)S(1)}, bf16[48,8,418]{2,1,0:T(8,128)(2,1)S(1)}, u32[]{:S(2)}, u32[]{:S(2)}) collective-permute-start(bf16[48,8,418]{2,1,0:T(8,128)(2,1)S(1)} %get-tuple-element.5), channel_id=1, source_target_pairs={{0,4},{1,5},{2,6},{3,7},{8,12},{9,13},{10,14},{11,15},{16,20},{17,... | collective-permute-start | bytes 963080 | tf_op jit(solution)/shard_map/ppermute | solution.py:23
  16.4 1.3 %collective-permute-start.8 = (bf16[48,8,418]{2,1,0:T(8,128)(2,1)S(1)}, bf16[48,8,418]{2,1,0:T(8,128)(2,1)S(1)}, u32[]{:S(2)}, u32[]{:S(2)}) collective-permute-start(bf16[48,8,418]{2,1,0:T(8,128)(2,1)S(1)} %get-tuple-element.6), channel_id=1, source_target_pairs={{4,0},{5,1},{6,2},{7,3},{12,8},{13,9},{14,10},{15,11},{20,16},{21,... | collective-permute-start | bytes 963080 | tf_op jit(solution)/shard_map/ppermute | solution.py:24
  17.7 0.0 collective-permute-done
  17.7 0.9 collective-permute-start.1
  18.6 0.0 copy-start.1
  18.6 1.2 %collective-permute-start.2 = (bf16[8,32,256]{2,1,0:T(8,128)(2,1)S(1)}, bf16[8,32,256]{2,1,0:T(8,128)(2,1)S(1)}, u32[]{:S(2)}, u32[]{:S(2)}) collective-permute-start(bf16[8,32,256]{2,1,0:T(8,128)(2,1)S(1)} %get-tuple-element.12), channel_id=1, source_target_pairs={{8,0},{16,8},{24,16},{0,24},{9,1},{17,9},{25,17},{1,25},{10,2},{18... | collective-permute-start | bytes 393224 | tf_op jit(solution)/shard_map/ppermute | solution.py:24
  19.8 5.9 %collective-permute-done.7 = bf16[48,8,418]{2,1,0:T(8,128)(2,1)S(1)} collective-permute-done((bf16[48,8,418]{2,1,0:T(8,128)(2,1)S(1)}, bf16[48,8,418]{2,1,0:T(8,128)(2,1)S(1)}, u32[]{:S(2)}, u32[]{:S(2)}) %collective-permute-start.7) | collective-permute-done | bytes 321056 | tf_op jit(solution)/shard_map/ppermute | solution.py:23
  25.7 4.4 %collective-permute-done.8 = bf16[48,8,418]{2,1,0:T(8,128)(2,1)S(1)} collective-permute-done((bf16[48,8,418]{2,1,0:T(8,128)(2,1)S(1)}, bf16[48,8,418]{2,1,0:T(8,128)(2,1)S(1)}, u32[]{:S(2)}, u32[]{:S(2)}) %collective-permute-start.8) | collective-permute-done | bytes 321056 | tf_op jit(solution)/shard_map/ppermute | solution.py:24
  30.1 0.0 copy-done.2
  30.1 0.0 copy-done
  30.1 2.2 %pad_maximum_fusion.ext_ref = bf16[48,48,418]{2,1,0:T(8,128)(2,1)S(1)} fusion(bf16[48,8,418]{2,1,0:T(8,128)(2,1)S(1)} %collective-permute-done.8, bf16[8,32,418]{2,1,0:T(8,128)(2,1)S(1)} %collective-permute-done.6, bf16[32,32,162]{2,1,0:T(8,128)(2,1)S(1)} %bitcast.11, bf16[32,32,256]{2,1,0:T(8,128)(2,1)S(1)} %bitcast.15, ...), kind=kLoop, calls=%fused_computation | loop fusion | flops 11556864 | bytes 3852288 | tf_op jit(solution)/shard_map/concatenate | solution.py:25
  32.4 0.0 collective-permute-done.1
  32.4 0.0 collective-permute-done.2
  32.4 1.5 %collective-permute-start.3 = (bf16[48,8,256]{2,1,0:T(8,128)(2,1)S(1)}, bf16[48,8,256]{2,1,0:T(8,128)(2,1)S(1)}, u32[]{:S(2)}, u32[]{:S(2)}) collective-permute-start(bf16[48,8,256]{2,1,0:T(8,128)(2,1)S(1)} %get-tuple-element.9), channel_id=1, source_target_pairs={{0,4},{1,5},{2,6},{3,7},{8,12},{9,13},{10,14},{11,15},{16,20},{17,... | collective-permute-start | bytes 589832 | tf_op jit(solution)/shard_map/ppermute | solution.py:23
  33.9 1.3 %collective-permute-start.4 = (bf16[48,8,256]{2,1,0:T(8,128)(2,1)S(1)}, bf16[48,8,256]{2,1,0:T(8,128)(2,1)S(1)}, u32[]{:S(2)}, u32[]{:S(2)}) collective-permute-start(bf16[48,8,256]{2,1,0:T(8,128)(2,1)S(1)} %get-tuple-element.10), channel_id=1, source_target_pairs={{4,0},{5,1},{6,2},{7,3},{12,8},{13,9},{14,10},{15,11},{20,16},{21,... | collective-permute-start | bytes 589832 | tf_op jit(solution)/shard_map/ppermute | solution.py:24
  35.2 0.0 copy-done.1
  35.2 29.0 %shard_map.38 = f32[32,32,256]{2,1,0:T(8,128)S(1)} custom-call(bf16[48,48,418]{2,1,0:T(8,128)(2,1)S(1)} %pad_maximum_fusion.ext_ref, bf16[162,1024]{1,0:T(8,128)(2,1)S(1)} %copy-done.1), custom_call_target="tpu_custom_call" | custom-call | flops 10000000000 | bytes 4194304 | tf_op jit(solution)/shard_map/pallas_call | solution.py:107
  64.2 4.6 %collective-permute-start.9 = (f32[32,32,256]{2,1,0:T(8,128)S(1)}, f32[32,32,256]{2,1,0:T(8,128)S(1)}, u32[]{:S(2)}, u32[]{:S(2)}) collective-permute-start(f32[32,32,256]{2,1,0:T(8,128)S(1)} %shard_map.38), channel_id=1, source_target_pairs={{0,1},{1,2},{2,3},{4,5},{5,6},{6,7},{8,9},{9,10},{10,11},{12,13},{... | collective-permute-start | bytes 3145736 | tf_op jit(solution)/shard_map/ppermute | solution.py:32
  68.8 0.0 collective-permute-done.3
  68.9 0.0 collective-permute-done.4
  68.9 0.1 pad_maximum_fusion.1.ext_ref
  69.0 14.9 %shard_map.37 = f32[32,32,256]{2,1,0:T(8,128)S(1)} custom-call(bf16[32,32,162]{2,1,0:T(8,128)(2,1)S(1)} %bitcast.12, bf16[48,48,256]{2,1,0:T(8,128)(2,1)S(1)} %pad_maximum_fusion.1.ext_ref, bf16[162,1024]{1,0:T(8,128)(2,1)S(1)} %copy-done.1), custom_call_target="tpu_custom_call" | custom-call | flops 10000000000 | bytes 4194304 | tf_op jit(solution)/shard_map/pallas_call | solution.py:107
  83.8 7.3 %collective-permute-done.9 = f32[32,32,256]{2,1,0:T(8,128)S(1)} collective-permute-done((f32[32,32,256]{2,1,0:T(8,128)S(1)}, f32[32,32,256]{2,1,0:T(8,128)S(1)}, u32[]{:S(2)}, u32[]{:S(2)}) %collective-permute-start.9) | collective-permute-done | bytes 1048608 | tf_op jit(solution)/shard_map/ppermute | solution.py:32
  91.1 1.0 %fusion = bf16[1,32,32,256]{3,2,1,0:T(8,128)(2,1)} fusion(f32[32,32,256]{2,1,0:T(8,128)S(1)} %shard_map.37, f32[32,32,256]{2,1,0:T(8,128)S(1)} %collective-permute-done.9), kind=kLoop, calls=%fused_computation.3 | loop fusion | flops 524288 | bytes 2621440 | tf_op jit(solution)/shard_map/broadcast_in_dim | solution.py:135
  (2 shorter events, 0.0 us)
Async XLA Ops:
  0.0 30.1 %copy-start.2 = (bf16[1,32,32,256]{3,2,1,0:T(8,128)(2,1)S(1)}, bf16[1,32,32,256]{3,2,1,0:T(8,128)(2,1)}, u32[]{:S(2)}) copy-start(bf16[1,32,32,256]{3,2,1,0:T(8,128)(2,1)} %param.3) | copy-start | bytes 1572868
  0.0 30.1 %copy-start = (bf16[1,32,32,162]{3,2,1,0:T(8,128)(2,1)S(1)}, bf16[1,32,32,162]{3,2,1,0:T(8,128)(2,1)}, u32[]{:S(2)}) copy-start(bf16[1,32,32,162]{3,2,1,0:T(8,128)(2,1)} %param.4) | copy-start | bytes 995332
  0.0 17.7 %collective-permute-start = (bf16[1,32,32,256]{3,2,1,0:T(8,128)(2,1)}, bf16[1,32,32,256]{3,2,1,0:T(8,128)(2,1)S(1)}, u32[]{:S(2)}, u32[]{:S(2)}) collective-permute-start(bf16[1,32,32,256]{3,2,1,0:T(8,128)(2,1)} %param.3), channel_id=1, source_target_pairs={{1,0},{2,1},{3,2},{5,4},{6,5},{7,6},{9,8},{10,9},{11,10},{13,12},{... | collective-permute-start | bytes 1572872 | tf_op jit(solution)/shard_map/ppermute | solution.py:32
  2.6 6.7 %collective-permute-start.5 = (bf16[8,32,418]{2,1,0:T(8,128)(2,1)S(1)}, bf16[8,32,418]{2,1,0:T(8,128)(2,1)S(1)}, u32[]{:S(2)}, u32[]{:S(2)}) collective-permute-start(bf16[8,32,418]{2,1,0:T(8,128)(2,1)S(1)} %get-tuple-element.7), channel_id=1, source_target_pairs={{0,8},{8,16},{16,24},{24,0},{1,9},{9,17},{17,25},{25,1},{2,10},{10... | collective-permute-start | bytes 642056 | tf_op jit(solution)/shard_map/ppermute | solution.py:23
  3.1 8.6 %collective-permute-start.6 = (bf16[8,32,418]{2,1,0:T(8,128)(2,1)S(1)}, bf16[8,32,418]{2,1,0:T(8,128)(2,1)S(1)}, u32[]{:S(2)}, u32[]{:S(2)}) collective-permute-start(bf16[8,32,418]{2,1,0:T(8,128)(2,1)S(1)} %get-tuple-element.8), channel_id=1, source_target_pairs={{8,0},{16,8},{24,16},{0,24},{9,1},{17,9},{25,17},{1,25},{10,2},{18... | collective-permute-start | bytes 642056 | tf_op jit(solution)/shard_map/ppermute | solution.py:24
  12.9 12.8 %collective-permute-start.7 = (bf16[48,8,418]{2,1,0:T(8,128)(2,1)S(1)}, bf16[48,8,418]{2,1,0:T(8,128)(2,1)S(1)}, u32[]{:S(2)}, u32[]{:S(2)}) collective-permute-start(bf16[48,8,418]{2,1,0:T(8,128)(2,1)S(1)} %get-tuple-element.5), channel_id=1, source_target_pairs={{0,4},{1,5},{2,6},{3,7},{8,12},{9,13},{10,14},{11,15},{16,20},{17,... | collective-permute-start | bytes 963080 | tf_op jit(solution)/shard_map/ppermute | solution.py:23
  16.4 13.7 %collective-permute-start.8 = (bf16[48,8,418]{2,1,0:T(8,128)(2,1)S(1)}, bf16[48,8,418]{2,1,0:T(8,128)(2,1)S(1)}, u32[]{:S(2)}, u32[]{:S(2)}) collective-permute-start(bf16[48,8,418]{2,1,0:T(8,128)(2,1)S(1)} %get-tuple-element.6), channel_id=1, source_target_pairs={{4,0},{5,1},{6,2},{7,3},{12,8},{13,9},{14,10},{15,11},{20,16},{21,... | collective-permute-start | bytes 963080 | tf_op jit(solution)/shard_map/ppermute | solution.py:24
  17.7 14.6 %collective-permute-start.1 = (bf16[8,32,256]{2,1,0:T(8,128)(2,1)S(1)}, bf16[8,32,256]{2,1,0:T(8,128)(2,1)S(1)}, u32[]{:S(2)}, u32[]{:S(2)}) collective-permute-start(bf16[8,32,256]{2,1,0:T(8,128)(2,1)S(1)} %get-tuple-element.11), channel_id=1, source_target_pairs={{0,8},{8,16},{16,24},{24,0},{1,9},{9,17},{17,25},{25,1},{2,10},{10... | collective-permute-start | bytes 393224 | tf_op jit(solution)/shard_map/ppermute | solution.py:23
  18.6 16.6 %copy-start.1 = (bf16[162,1024]{1,0:T(8,128)(2,1)S(1)}, bf16[162,1024]{1,0:T(8,128)(2,1)}, u32[]{:S(2)}) copy-start(bf16[162,1024]{1,0:T(8,128)(2,1)} %constant.5.spread_ref) | copy-start | bytes 995332
  18.6 13.8 %collective-permute-start.2 = (bf16[8,32,256]{2,1,0:T(8,128)(2,1)S(1)}, bf16[8,32,256]{2,1,0:T(8,128)(2,1)S(1)}, u32[]{:S(2)}, u32[]{:S(2)}) collective-permute-start(bf16[8,32,256]{2,1,0:T(8,128)(2,1)S(1)} %get-tuple-element.12), channel_id=1, source_target_pairs={{8,0},{16,8},{24,16},{0,24},{9,1},{17,9},{25,17},{1,25},{10,2},{18... | collective-permute-start | bytes 393224 | tf_op jit(solution)/shard_map/ppermute | solution.py:24
  32.4 36.4 %collective-permute-start.3 = (bf16[48,8,256]{2,1,0:T(8,128)(2,1)S(1)}, bf16[48,8,256]{2,1,0:T(8,128)(2,1)S(1)}, u32[]{:S(2)}, u32[]{:S(2)}) collective-permute-start(bf16[48,8,256]{2,1,0:T(8,128)(2,1)S(1)} %get-tuple-element.9), channel_id=1, source_target_pairs={{0,4},{1,5},{2,6},{3,7},{8,12},{9,13},{10,14},{11,15},{16,20},{17,... | collective-permute-start | bytes 589832 | tf_op jit(solution)/shard_map/ppermute | solution.py:23
  33.9 35.0 %collective-permute-start.4 = (bf16[48,8,256]{2,1,0:T(8,128)(2,1)S(1)}, bf16[48,8,256]{2,1,0:T(8,128)(2,1)S(1)}, u32[]{:S(2)}, u32[]{:S(2)}) collective-permute-start(bf16[48,8,256]{2,1,0:T(8,128)(2,1)S(1)} %get-tuple-element.10), channel_id=1, source_target_pairs={{4,0},{5,1},{6,2},{7,3},{12,8},{13,9},{14,10},{15,11},{20,16},{21,... | collective-permute-start | bytes 589832 | tf_op jit(solution)/shard_map/ppermute | solution.py:24
  64.2 26.9 %collective-permute-start.9 = (f32[32,32,256]{2,1,0:T(8,128)S(1)}, f32[32,32,256]{2,1,0:T(8,128)S(1)}, u32[]{:S(2)}, u32[]{:S(2)}) collective-permute-start(f32[32,32,256]{2,1,0:T(8,128)S(1)} %shard_map.38), channel_id=1, source_target_pairs={{0,1},{1,2},{2,3},{4,5},{5,6},{6,7},{8,9},{9,10},{10,11},{12,13},{... | collective-permute-start | bytes 3145736 | tf_op jit(solution)/shard_map/ppermute | solution.py:32
where the time goes:
time: 92.7 us; the launch traced here: 92.1 us
  Pallas kernels  43.9 us (47%)
  waiting for transfers between devices  24.3 us (26%)
  starting transfers between devices  18.1 us (20%)
  other arithmetic  5.65 us (6%)
    pallas_call x2, Pallas kernels, local_call(): pl.pallas_call(kernel, out_shape=jax.ShapeDtypeStruct((cols, rows, chans)...  43.9 us
    ppermute x4, waiting for transfers between devices, extended_2(): before = lax.ppermute(last, axis, up)  10.1 us
    ppermute x2, waiting for transfers between devices, from_behind(): lax.ppermute(value, axis, [(source, source + steps) for source in range(f...  7.31 us
    ppermute x4, waiting for transfers between devices, extended_2(): after = lax.ppermute(first, axis, down)  6.83 us
    ppermute x4, starting transfers between devices, extended_2(): before = lax.ppermute(last, axis, up)  6.33 us
    ppermute x2, starting transfers between devices, from_behind(): lax.ppermute(value, axis, [(source, source + steps) for source in range(f...  6.05 us
    ppermute x4, starting transfers between devices, extended_2(): after = lax.ppermute(first, axis, down)  5.73 us
    slice x3, other arithmetic, extended_2(): last = lax.slice_in_dim(array, length - width, length, axis=dim)  2.38 us
  transfers between devices with their start and end apart: 10, of which 5 were waited for; matrix products, arithmetic and copies ran while one was open for 5% of the time, Pallas kernels for 48%

commit v1 on v0

v1 whole, which is shorter than its diff:
```python
import jax
import jax.numpy as jnp
import numpy as np
from jax import lax
from jax.experimental import pallas as pl
from jax.experimental.pallas import tpu as pltpu
from jax.sharding import PartitionSpec as P

LEVELS = 2
RAD = 4
RIM = 8
ACROSS = 2 * RAD + 1
BLOCK = 4


def extended(array, axis, dim, wrap):
    size, length = (lax.axis_size(axis), array.shape[dim])
    last = lax.slice_in_dim(array, length - RIM, length, axis=dim)
    first = lax.slice_in_dim(array, 0, RIM, axis=dim)
    if size == 2 and not wrap:
        lower = lax.axis_index(axis) == 0
        met = lax.ppermute(jnp.where(lower, last, first), axis, [(0, 1), (1, 0)])
        none = jnp.zeros_like(met)
        before, after = jnp.where(lower, none, met), jnp.where(lower, met, none)
    else:
        up = [(i, (i + 1) % size) for i in range(size if wrap else size - 1)]
        before = lax.ppermute(last, axis, up)
        after = lax.ppermute(first, axis, [(j, i) for i, j in up])
    return jnp.concatenate([before, array, after], axis=dim)


def from_behind(value, axis, steps):
    count = lax.axis_size(axis)
    first, last = (max(0, -steps), min(count, count - steps))
    return lax.ppermute(value, axis, [(source, source + steps) for source in range(first, last)])


def spreader(rows, starts, lanes):
    out = np.zeros((LEVELS * ACROSS * ACROSS, sum(lanes)), np.float32)
    for a in range(ACROSS):
        for b in range(ACROSS):
            out[a * ACROSS + b, a * starts[0] * rows + RAD + b] = 1
            out[ACROSS * ACROSS + a * ACROSS + b, lanes[0] + a * starts[1] * rows + 2 * b] = 1
    return jnp.asarray(out).astype(jnp.bfloat16)


def sheared(spread, rows, shifts):
    parts = [
        pltpu.roll(spread[i * rows : (i + 1) * rows], shift, 1, stride=1, stride_axis=0)
        for i, shift in enumerate(shifts)
    ]
    return jnp.concatenate(parts, axis=0).astype(jnp.bfloat16)


def pair_sum(value):
    rows = value.shape[0]
    odd = lax.broadcasted_iota(jnp.int32, value.shape, 0) % 2 == 1
    return value + jnp.where(odd, pltpu.roll(value, 1, 0), pltpu.roll(value, rows - 1, 0))


def padded(lanes):
    return -(-lanes // 128) * 128


def own_lanes(wide):
    return padded((ACROSS + BLOCK - 1) * wide), padded((ACROSS + BLOCK // 2 - 1) * wide)


def back_lanes(wide):
    return padded((ACROSS + BLOCK - 1) * wide), padded((2 * ACROSS + BLOCK - 2) * wide)


def own_kernel(cot_ref, ext_ref, spread_ref, out_ref, pool_ref):
    cols, rows, chans = out_ref.shape
    wide = rows + 2 * RIM
    lanes = own_lanes(wide)
    near_cols, far_cols = ACROSS + BLOCK - 1, ACROSS + BLOCK // 2 - 1

    @pl.loop(0, (cols + 2 * RIM) // 2)
    def _(pos):
        both = ext_ref[2 * pos].astype(jnp.float32) + ext_ref[2 * pos + 1].astype(jnp.float32)
        pool_ref[pos] = (pair_sum(both) * 0.25).astype(jnp.bfloat16)

    @pl.loop(0, cols // BLOCK)
    def _(pos):
        x = pos * BLOCK
        cot = cot_ref[pl.ds(x, BLOCK)].reshape(BLOCK * rows, cot_ref.shape[2])
        spread = jnp.dot(cot, spread_ref[...], preferred_element_type=jnp.float32)
        near = sheared(spread[:, : lanes[0]], rows, [i * wide for i in range(BLOCK)])
        far = sheared(spread[:, lanes[0] :], rows, [i // 2 * wide for i in range(BLOCK)])
        keys = ext_ref[pl.ds(x + RAD, near_cols)].reshape(near_cols * wide, chans)
        pooled = pool_ref[pl.ds(pos * (BLOCK // 2), far_cols)].reshape(far_cols * wide, chans)
        total = jnp.dot(near[:, : near_cols * wide], keys, preferred_element_type=jnp.float32)
        total = total + jnp.dot(far[:, : far_cols * wide], pooled, preferred_element_type=jnp.float32)
        out_ref[pl.ds(x, BLOCK)] = (total * chans ** (-0.5)).reshape(BLOCK, rows, chans)


def back_kernel(ext_ref, spread_ref, out_ref, near_ref, far_ref):
    cols, rows, chans = out_ref.shape
    wide = rows + 2 * RIM
    lanes = back_lanes(wide)
    contract = (((0,), (0,)), ((), ()))

    @pl.loop(0, cols + 4 * RIM)
    def _(pos):
        near_ref[pos] = jnp.zeros((rows, chans), jnp.float32)
        far_ref[pos] = jnp.zeros((rows, chans), jnp.float32)

    @pl.loop(0, (cols + 2 * RIM) // BLOCK)
    def _(pos):
        x = pos * BLOCK
        feats = ext_ref[pl.ds(x, BLOCK), :, :chans].reshape(BLOCK * wide, chans)
        cot = ext_ref[pl.ds(x, BLOCK), :, chans:]
        cot = cot.reshape(BLOCK * wide, cot.shape[2])
        spread = jnp.dot(cot, spread_ref[...], preferred_element_type=jnp.float32)
        shifts = [i * wide for i in range(BLOCK)]
        near = sheared(spread[:, : lanes[0]], wide, shifts)
        far = sheared(spread[:, lanes[0] :], wide, shifts)
        near = lax.dot_general(near, feats, contract, preferred_element_type=jnp.float32)
        far = lax.dot_general(far, feats, contract, preferred_element_type=jnp.float32)
        for k in range(ACROSS + BLOCK - 1):
            begin = k * wide + 2 * RIM
            near_ref[x + k + RAD] += near[begin : begin + rows]
        for k in range(2 * ACROSS + BLOCK - 2):
            begin = k * wide + 2 * RIM
            far_ref[x + k] += far[begin : begin + rows]

    @pl.loop(0, cols // 2)
    def _(pos):
        u = 2 * pos + 2 * RIM
        both = pair_sum(far_ref[u] + far_ref[u + 1]) * 0.25
        out_ref[2 * pos] = (near_ref[u] + both) * chans ** (-0.5)
        out_ref[2 * pos + 1] = (near_ref[u + 1] + both) * chans ** (-0.5)


def local_call(kernel, cols, rows, chans, scratch, flops, *args):
    vmem = pl.BlockSpec(memory_space=pltpu.VMEM)
    return pl.pallas_call(
        kernel,
        out_shape=jax.ShapeDtypeStruct((cols, rows, chans), jnp.float32),
        in_specs=[vmem] * len(args),
        out_specs=vmem,
        scratch_shapes=scratch,
        cost_estimate=pl.CostEstimate(flops=flops, bytes_accessed=4 << 20, transcendentals=0),
        compiler_params=pltpu.CompilerParams(vmem_limit_bytes=40 << 20),
    )(*args)


def extend(stacked):
    return extended(extended(stacked, "lon", 0, True), "lat", 1, False)


def body(features, cotangent):
    _, cols, rows, chans = features.shape
    wide = rows + 2 * RIM
    back_spread = spreader(wide, (1, 2), back_lanes(wide))
    own_spread = spreader(wide, (1, 1), own_lanes(wide))
    following = from_behind(features, "frame", -1)
    query_ext = extend(jnp.concatenate([features[0], cotangent[0]], axis=2))
    next_ext = extend(following[0])
    wider = pltpu.VMEM((cols + 4 * RIM, rows, chans), jnp.float32)
    key_part = local_call(back_kernel, cols, rows, chans, [wider, wider], 10**10, query_ext, back_spread)
    carried = from_behind(key_part, "frame", 1)
    pool = pltpu.VMEM((cols // 2 + RIM, wide, chans), jnp.bfloat16)
    own = local_call(own_kernel, cols, rows, chans, [pool], 10**10, cotangent[0], next_ext, own_spread)
    return (own + carried).astype(jnp.bfloat16)[None]


def solution(mesh):
    placed = (P("frame", "lon", "lat", None), P("frame", "lon", "lat", None))
    return jax.shard_map(
        body, mesh=mesh, in_specs=placed, out_specs=P("frame", "lon", "lat", None), check_vma=False
    )
```

time: 92.7 us -> 69.5 us (0.75)
  Pallas kernels: 43.9 us -> 17.8 us
  waiting for transfers between devices: 24.3 us -> 32.1 us
  starting transfers between devices: 18.1 us -> 13.4 us
    pallas_call x2, Pallas kernels: 43.9 us -> 17.8 us  [local_call(): pl.pallas_call(kernel, out_shape=jax.ShapeDtypeStruct((cols, rows, chans)...]
    ppermute x2, waiting for transfers between devices: 7.31 us -> 19.4 us  [from_behind(): lax.ppermute(value, axis, [(source, source + steps) for source in range(f...]
    ppermute x8 -> x6, starting transfers between devices: 12.1 us -> 7.43 us  [the longest x2 3.71 us: extended(): after = lax.ppermute(first, axis, [(j, i) for i, j in up])]
    ppermute x8 -> x6, waiting for transfers between devices: 17 us -> 12.6 us  [the longest x2 5.99 us: extended(): met = lax.ppermute(jnp.where(lower, last, first), axis, [(0, 1), (1, 0)])]
    select_n x0 -> x4, other arithmetic: none -> 1.35 us  [the longest x2 1.26 us: extended(): met = lax.ppermute(jnp.where(lower, last, first), axis, [(0, 1), (1, 0)])]
    slice x3 -> x1, other arithmetic: 2.38 us -> 1.24 us  [extended(): last = lax.slice_in_dim(array, length - RIM, length, axis=dim)]
  transfers between devices with their start and end apart: 10 -> 8, of which waited for: 5 -> 5; matrix products, arithmetic and copies ran while one was open for 5% -> 7% of each run, Pallas kernels for 48% -> 26%
where the time goes in v1:
time: 69.5 us; the launch traced here: 69.3 us
  waiting for transfers between devices  32.1 us (46%)
  Pallas kernels  17.8 us (26%)
  starting transfers between devices  13.4 us (19%)
  other arithmetic  5.9 us (8%)
    ppermute x2, waiting for transfers between devices, from_behind(): lax.ppermute(value, axis, [(source, source + steps) for source in range(f...  19.4 us
    pallas_call x2, Pallas kernels, local_call(): pl.pallas_call(kernel, out_shape=jax.ShapeDtypeStruct((cols, rows, chans)...  17.8 us
    ppermute x2, waiting for transfers between devices, extended(): met = lax.ppermute(jnp.where(lower, last, first), axis, [(0, 1), (1, 0)])  5.99 us
    ppermute x2, starting transfers between devices, from_behind(): lax.ppermute(value, axis, [(source, source + steps) for source in range(f...  5.93 us
    ppermute x2, waiting for transfers between devices, extended(): before = lax.ppermute(last, axis, up)  4.2 us
    ppermute x2, starting transfers between devices, extended(): after = lax.ppermute(first, axis, [(j, i) for i, j in up])  3.71 us
    ppermute x2, starting transfers between devices, extended(): met = lax.ppermute(jnp.where(lower, last, first), axis, [(0, 1), (1, 0)])  3.12 us
    ppermute x2, waiting for transfers between devices, extended(): after = lax.ppermute(first, axis, [(j, i) for i, j in up])  2.42 us
  transfers between devices with their start and end apart: 8, of which 5 were waited for; matrix products, arithmetic and copies ran while one was open for 7% of the time, Pallas kernels for 26%

profile of v1, /device:TPU:0, one launch (start us, length us, event | category | flops | bytes accessed | tf_op | source)
XLA Modules:
  0.0 69.3 jit_solution(17276648274528549848)
XLA Ops:
  0.0 1.3 %collective-permute-start = (bf16[1,32,32,256]{3,2,1,0:T(8,128)(2,1)}, bf16[1,32,32,256]{3,2,1,0:T(8,128)(2,1)S(1)}, u32[]{:S(2)}, u32[]{:S(2)}) collective-permute-start(bf16[1,32,32,256]{3,2,1,0:T(8,128)(2,1)} %param.4), channel_id=1, source_target_pairs={{1,0},{2,1},{3,2},{5,4},{6,5},{7,6},{9,8},{10,9},{11,10},{13,12},{... | collective-permute-start | bytes 1572872 | tf_op jit(solution)/shard_map/ppermute | solution.py:35
  1.3 0.0 copy-start
  1.3 0.0 copy-start.3
  1.3 1.2 %pad_maximum_fusion.6 = (bf16[8,32,418]{2,1,0:T(8,128)(2,1)S(1)}, bf16[8,32,418]{2,1,0:T(8,128)(2,1)S(1)}) fusion(bf16[32,32,162]{2,1,0:T(8,128)(2,1)} %bitcast.9, bf16[32,32,256]{2,1,0:T(8,128)(2,1)} %bitcast.13), kind=kLoop, calls=%fused_computation.11 | loop fusion | flops 856064 | bytes 1284096 | tf_op jit(solution)/shard_map/slice | solution.py:18
  2.6 0.5 collective-permute-start.4
  3.1 2.0 %collective-permute-start.5 = (bf16[8,32,418]{2,1,0:T(8,128)(2,1)S(1)}, bf16[8,32,418]{2,1,0:T(8,128)(2,1)S(1)}, u32[]{:S(2)}, u32[]{:S(2)}) collective-permute-start(bf16[8,32,418]{2,1,0:T(8,128)(2,1)S(1)} %get-tuple-element.6), channel_id=1, source_target_pairs={{8,0},{16,8},{24,16},{0,24},{9,1},{17,9},{25,17},{1,25},{10,2},{18... | collective-permute-start | bytes 642056 | tf_op jit(solution)/shard_map/ppermute | solution.py:28
  5.1 4.2 %collective-permute-done.4 = bf16[8,32,418]{2,1,0:T(8,128)(2,1)S(1)} collective-permute-done((bf16[8,32,418]{2,1,0:T(8,128)(2,1)S(1)}, bf16[8,32,418]{2,1,0:T(8,128)(2,1)S(1)}, u32[]{:S(2)}, u32[]{:S(2)}) %collective-permute-start.4) | collective-permute-done | bytes 214048 | tf_op jit(solution)/shard_map/ppermute | solution.py:27
  9.3 2.4 %collective-permute-done.5 = bf16[8,32,418]{2,1,0:T(8,128)(2,1)S(1)} collective-permute-done((bf16[8,32,418]{2,1,0:T(8,128)(2,1)S(1)}, bf16[8,32,418]{2,1,0:T(8,128)(2,1)S(1)}, u32[]{:S(2)}, u32[]{:S(2)}) %collective-permute-start.5) | collective-permute-done | bytes 214048 | tf_op jit(solution)/shard_map/ppermute | solution.py:28
  11.7 1.2 %fusion.1 = bf16[48,8,418]{2,1,0:T(8,128)(2,1)S(1)} fusion(bf16[8,32,418]{2,1,0:T(8,128)(2,1)S(1)} %collective-permute-done.5, bf16[8,32,418]{2,1,0:T(8,128)(2,1)S(1)} %collective-permute-done.4, bf16[32,32,162]{2,1,0:T(8,128)(2,1)} %bitcast.10, bf16[32,32,256]{2,1,0:T(8,128)(2,1)} %bitcast.14, pred[]{:T(512)S(6)} %eq.4), kind=kLoop, calls=%fused_computation.5 | loop fusion | flops 2728704 | bytes 1605121 | tf_op jit(solution)/shard_map/jit(_where)/select_n | solution.py:22
  12.9 1.6 %collective-permute-start.6 = (bf16[48,8,418]{2,1,0:T(8,128)(2,1)S(1)}, bf16[48,8,418]{2,1,0:T(8,128)(2,1)S(1)}, u32[]{:S(2)}, u32[]{:S(2)}) collective-permute-start(bf16[48,8,418]{2,1,0:T(8,128)(2,1)S(1)} %fusion.1), channel_id=1, source_target_pairs={{0,4},{4,0},{1,5},{5,1},{2,6},{6,2},{3,7},{7,3},{8,12},{12,8},{9,1... | collective-permute-start | bytes 963080 | tf_op jit(solution)/shard_map/ppermute | solution.py:22
  14.5 2.6 %collective-permute-done = bf16[1,32,32,256]{3,2,1,0:T(8,128)(2,1)S(1)} collective-permute-done((bf16[1,32,32,256]{3,2,1,0:T(8,128)(2,1)}, bf16[1,32,32,256]{3,2,1,0:T(8,128)(2,1)S(1)}, u32[]{:S(2)}, u32[]{:S(2)}) %collective-permute-start) | collective-permute-done | bytes 524320 | tf_op jit(solution)/shard_map/ppermute | solution.py:35
  17.1 0.1 collective-permute-start.1
  17.2 1.7 %collective-permute-start.2 = (bf16[8,32,256]{2,1,0:T(8,128)(2,1)S(1)}, bf16[8,32,256]{2,1,0:T(8,128)(2,1)S(1)}, u32[]{:S(2)}, u32[]{:S(2)}) collective-permute-start(bf16[8,32,256]{2,1,0:T(8,128)(2,1)S(1)} %get-tuple-element.8), channel_id=1, source_target_pairs={{8,0},{16,8},{24,16},{0,24},{9,1},{17,9},{25,17},{1,25},{10,2},{18... | collective-permute-start | bytes 393224 | tf_op jit(solution)/shard_map/ppermute | solution.py:28
  18.9 6.0 %collective-permute-done.6 = bf16[48,8,418]{2,1,0:T(8,128)(2,1)S(1)} collective-permute-done((bf16[48,8,418]{2,1,0:T(8,128)(2,1)S(1)}, bf16[48,8,418]{2,1,0:T(8,128)(2,1)S(1)}, u32[]{:S(2)}, u32[]{:S(2)}) %collective-permute-start.6) | collective-permute-done | bytes 321056 | tf_op jit(solution)/shard_map/ppermute | solution.py:22
  24.9 0.1 broadcast_select_fusion.1
  24.9 0.0 copy-done
  25.0 0.0 copy-done.3
  25.0 0.0 copy-start.1
  25.0 2.3 %pad_maximum_fusion.ext_ref = bf16[48,48,418]{2,1,0:T(8,128)(2,1)S(1)} fusion(bf16[48,8,418]{2,1,0:T(8,128)(2,1)S(1)} %get-tuple-element.10, bf16[8,32,418]{2,1,0:T(8,128)(2,1)S(1)} %collective-permute-done.5, bf16[32,32,162]{2,1,0:T(8,128)(2,1)S(1)} %bitcast.11, bf16[32,32,256]{2,1,0:T(8,128)(2,1)S(1)} %bitcast.15, ...), kind=kLoop, calls=%fused_computation | loop fusion | flops 11556864 | bytes 3852288 | tf_op jit(solution)/shard_map/concatenate | solution.py:29
  27.3 0.0 collective-permute-done.1
  27.3 0.0 collective-permute-done.2
  27.3 0.1 fusion.2
  27.3 1.5 %collective-permute-start.3 = (bf16[48,8,256]{2,1,0:T(8,128)(2,1)S(1)}, bf16[48,8,256]{2,1,0:T(8,128)(2,1)S(1)}, u32[]{:S(2)}, u32[]{:S(2)}) collective-permute-start(bf16[48,8,256]{2,1,0:T(8,128)(2,1)S(1)} %fusion.2), channel_id=1, source_target_pairs={{0,4},{4,0},{1,5},{5,1},{2,6},{6,2},{3,7},{7,3},{8,12},{12,8},{9,1... | collective-permute-start | bytes 589832 | tf_op jit(solution)/shard_map/ppermute | solution.py:22
  28.9 0.0 copy-done.1
  28.9 12.5 %shard_map.47 = f32[32,32,256]{2,1,0:T(8,128)S(1)} custom-call(bf16[48,48,418]{2,1,0:T(8,128)(2,1)S(1)} %pad_maximum_fusion.ext_ref, bf16[162,1664]{1,0:T(8,128)(2,1)S(1)} %copy-done.1), custom_call_target="tpu_custom_call" | custom-call | flops 10000000000 | bytes 4194304 | tf_op jit(solution)/shard_map/pallas_call | solution.py:138
  41.4 0.0 copy-start.2
  41.4 4.7 %collective-permute-start.7 = (f32[32,32,256]{2,1,0:T(8,128)S(1)}, f32[32,32,256]{2,1,0:T(8,128)S(1)}, u32[]{:S(2)}, u32[]{:S(2)}) collective-permute-start(f32[32,32,256]{2,1,0:T(8,128)S(1)} %shard_map.47), channel_id=1, source_target_pairs={{0,1},{1,2},{2,3},{4,5},{5,6},{6,7},{8,9},{9,10},{10,11},{12,13},{... | collective-permute-start | bytes 3145736 | tf_op jit(solution)/shard_map/ppermute | solution.py:35
  46.1 0.0 collective-permute-done.3
  46.1 0.1 pad_maximum_fusion.1.ext_ref
  46.2 0.0 copy-done.2
  46.2 5.3 %shard_map.46 = f32[32,32,256]{2,1,0:T(8,128)S(1)} custom-call(bf16[32,32,162]{2,1,0:T(8,128)(2,1)S(1)} %bitcast.12, bf16[48,48,256]{2,1,0:T(8,128)(2,1)S(1)} %pad_maximum_fusion.1.ext_ref, bf16[162,1152]{1,0:T(8,128)(2,1)S(1)} %copy-done.2), custom_call_target="tpu_custom_call" | custom-call | flops 10000000000 | bytes 4194304 | tf_op jit(solution)/shard_map/pallas_call | solution.py:138
  51.5 16.9 %collective-permute-done.7 = f32[32,32,256]{2,1,0:T(8,128)S(1)} collective-permute-done((f32[32,32,256]{2,1,0:T(8,128)S(1)}, f32[32,32,256]{2,1,0:T(8,128)S(1)}, u32[]{:S(2)}, u32[]{:S(2)}) %collective-permute-start.7) | collective-permute-done | bytes 1048608 | tf_op jit(solution)/shard_map/ppermute | solution.py:35
  68.4 1.0 %fusion = bf16[1,32,32,256]{3,2,1,0:T(8,128)(2,1)} fusion(f32[32,32,256]{2,1,0:T(8,128)S(1)} %shard_map.46, f32[32,32,256]{2,1,0:T(8,128)S(1)} %collective-permute-done.7), kind=kLoop, calls=%fused_computation.3 | loop fusion | flops 524288 | bytes 2621440 | tf_op jit(solution)/shard_map/broadcast_in_dim | solution.py:166
  (2 shorter events, 0.1 us)
Async XLA Ops:
  0.0 17.1 %collective-permute-start = (bf16[1,32,32,256]{3,2,1,0:T(8,128)(2,1)}, bf16[1,32,32,256]{3,2,1,0:T(8,128)(2,1)S(1)}, u32[]{:S(2)}, u32[]{:S(2)}) collective-permute-start(bf16[1,32,32,256]{3,2,1,0:T(8,128)(2,1)} %param.4), channel_id=1, source_target_pairs={{1,0},{2,1},{3,2},{5,4},{6,5},{7,6},{9,8},{10,9},{11,10},{13,12},{... | collective-permute-start | bytes 1572872 | tf_op jit(solution)/shard_map/ppermute | solution.py:35
  1.3 23.7 %copy-start = (bf16[1,32,32,162]{3,2,1,0:T(8,128)(2,1)S(1)}, bf16[1,32,32,162]{3,2,1,0:T(8,128)(2,1)}, u32[]{:S(2)}) copy-start(bf16[1,32,32,162]{3,2,1,0:T(8,128)(2,1)} %param.5) | copy-start | bytes 995332
  1.3 23.7 %copy-start.3 = (bf16[1,32,32,256]{3,2,1,0:T(8,128)(2,1)S(1)}, bf16[1,32,32,256]{3,2,1,0:T(8,128)(2,1)}, u32[]{:S(2)}) copy-start(bf16[1,32,32,256]{3,2,1,0:T(8,128)(2,1)} %param.4) | copy-start | bytes 1572868
  2.6 6.7 %collective-permute-start.4 = (bf16[8,32,418]{2,1,0:T(8,128)(2,1)S(1)}, bf16[8,32,418]{2,1,0:T(8,128)(2,1)S(1)}, u32[]{:S(2)}, u32[]{:S(2)}) collective-permute-start(bf16[8,32,418]{2,1,0:T(8,128)(2,1)S(1)} %get-tuple-element.5), channel_id=1, source_target_pairs={{0,8},{8,16},{16,24},{24,0},{1,9},{9,17},{17,25},{25,1},{2,10},{10... | collective-permute-start | bytes 642056 | tf_op jit(solution)/shard_map/ppermute | solution.py:27
  3.1 8.6 %collective-permute-start.5 = (bf16[8,32,418]{2,1,0:T(8,128)(2,1)S(1)}, bf16[8,32,418]{2,1,0:T(8,128)(2,1)S(1)}, u32[]{:S(2)}, u32[]{:S(2)}) collective-permute-start(bf16[8,32,418]{2,1,0:T(8,128)(2,1)S(1)} %get-tuple-element.6), channel_id=1, source_target_pairs={{8,0},{16,8},{24,16},{0,24},{9,1},{17,9},{25,17},{1,25},{10,2},{18... | collective-permute-start | bytes 642056 | tf_op jit(solution)/shard_map/ppermute | solution.py:28
  12.9 12.0 %collective-permute-start.6 = (bf16[48,8,418]{2,1,0:T(8,128)(2,1)S(1)}, bf16[48,8,418]{2,1,0:T(8,128)(2,1)S(1)}, u32[]{:S(2)}, u32[]{:S(2)}) collective-permute-start(bf16[48,8,418]{2,1,0:T(8,128)(2,1)S(1)} %fusion.1), channel_id=1, source_target_pairs={{0,4},{4,0},{1,5},{5,1},{2,6},{6,2},{3,7},{7,3},{8,12},{12,8},{9,1... | collective-permute-start | bytes 963080 | tf_op jit(solution)/shard_map/ppermute | solution.py:22
  17.1 10.2 %collective-permute-start.1 = (bf16[8,32,256]{2,1,0:T(8,128)(2,1)S(1)}, bf16[8,32,256]{2,1,0:T(8,128)(2,1)S(1)}, u32[]{:S(2)}, u32[]{:S(2)}) collective-permute-start(bf16[8,32,256]{2,1,0:T(8,128)(2,1)S(1)} %get-tuple-element.7), channel_id=1, source_target_pairs={{0,8},{8,16},{16,24},{24,0},{1,9},{9,17},{17,25},{25,1},{2,10},{10... | collective-permute-start | bytes 393224 | tf_op jit(solution)/shard_map/ppermute | solution.py:27
  17.2 10.1 %collective-permute-start.2 = (bf16[8,32,256]{2,1,0:T(8,128)(2,1)S(1)}, bf16[8,32,256]{2,1,0:T(8,128)(2,1)S(1)}, u32[]{:S(2)}, u32[]{:S(2)}) collective-permute-start(bf16[8,32,256]{2,1,0:T(8,128)(2,1)S(1)} %get-tuple-element.8), channel_id=1, source_target_pairs={{8,0},{16,8},{24,16},{0,24},{9,1},{17,9},{25,17},{1,25},{10,2},{18... | collective-permute-start | bytes 393224 | tf_op jit(solution)/shard_map/ppermute | solution.py:28
  25.0 3.9 %copy-start.1 = (bf16[162,1664]{1,0:T(8,128)(2,1)S(1)}, bf16[162,1664]{1,0:T(8,128)(2,1)}, u32[]{:S(2)}) copy-start(bf16[162,1664]{1,0:T(8,128)(2,1)} %constant.20.spread_ref) | copy-start | bytes 1617412
  27.3 18.7 %collective-permute-start.3 = (bf16[48,8,256]{2,1,0:T(8,128)(2,1)S(1)}, bf16[48,8,256]{2,1,0:T(8,128)(2,1)S(1)}, u32[]{:S(2)}, u32[]{:S(2)}) collective-permute-start(bf16[48,8,256]{2,1,0:T(8,128)(2,1)S(1)} %fusion.2), channel_id=1, source_target_pairs={{0,4},{4,0},{1,5},{5,1},{2,6},{6,2},{3,7},{7,3},{8,12},{12,8},{9,1... | collective-permute-start | bytes 589832 | tf_op jit(solution)/shard_map/ppermute | solution.py:22
  41.4 4.8 %copy-start.2 = (bf16[162,1152]{1,0:T(8,128)(2,1)S(1)}, bf16[162,1152]{1,0:T(8,128)(2,1)}, u32[]{:S(2)}) copy-start(bf16[162,1152]{1,0:T(8,128)(2,1)} %constant.19.spread_ref) | copy-start | bytes 1119748
  41.4 27.0 %collective-permute-start.7 = (f32[32,32,256]{2,1,0:T(8,128)S(1)}, f32[32,32,256]{2,1,0:T(8,128)S(1)}, u32[]{:S(2)}, u32[]{:S(2)}) collective-permute-start(f32[32,32,256]{2,1,0:T(8,128)S(1)} %shard_map.47), channel_id=1, source_target_pairs={{0,1},{1,2},{2,3},{4,5},{5,6},{6,7},{8,9},{9,10},{10,11},{12,13},{... | collective-permute-start | bytes 3145736 | tf_op jit(solution)/shard_map/ppermute | solution.py:35
